TPU v7x, 32 devices: a whole 2x2x4 slice. The times are simulated.
32 devices in a mesh: ctx: 16 (over z, y, x), head: 2 (over core).
Axes of the slice: x: 2, y: 2, z: 4, core: 2. Of those that a mesh axis runs over, the one named last changes fastest.
Arguments:
- queries: bfloat16 [2, 4096, 2048], P(None, 'ctx', 'head'), may hold values from -6 to 6
- key_vectors: bfloat16 [2, 4096, 2048], P(None, 'ctx', 'head'), may hold values from -0.4 to 0.4
- value_vectors: bfloat16 [2, 4096, 2048], P(None, 'ctx', 'head'), may hold values from -6 to 6
- log_decay: float32 [16, 2, 4096], P('head', None, 'ctx'), may hold values from -1 to 0
- ridge_shift: float32 [16], P('head'), may hold values from 0.25 to 4
- norm_gain: float32 [2048], P('head'), may hold values from 0.1 to 1.9
- out_weight: bfloat16 [2048, 4096], P(None, 'head'), may hold values from -0.125 to 0.125
Outputs:
- mixed: bfloat16 [2, 4096, 4096], P(None, 'ctx', 'head')
All inputs are finite; a program needn't handle non-finite values.
Results may differ from a plain program's by a relative error of at most 0.007.
Values may be sent and summed in bfloat16 or wider, within the bound.
No kernel may reach another device: no remote copies, remote signals or barrier semaphores. Data moves between devices by JAX's collectives and lax.ppermute only.
A program may use at most 128 MiB of HBM per device.

v0:
```python
import jax
import jax.numpy as jnp
from jax import lax
from jax.sharding import PartitionSpec as P

DK = 128
DV = 128
GROUP = 256
ITERS = 2
exact_mode = lax.Precision.HIGHEST
norm_epsilon = 1e-06
solve_epsilon = 1e-06


def entering_2(value, axis, join, neutral):
    count, mine = (lax.axis_size(axis), lax.axis_index(axis))
    pieces = jax.tree.map(lambda part: lax.all_gather(part, axis), value)
    total = jax.tree.map(
        lambda part, zero: jnp.full_like(part, 0) + jnp.asarray(zero, part.dtype), value, neutral
    )

    def lap(position, total):
        longer = join(total, jax.tree.map(lambda part: part[position], pieces))
        return jax.tree.map(lambda new, old: jnp.where(position < mine, new, old), longer, total)

    return lax.fori_loop(0, count - 1, lap, total)


def for_sending(shard):
    return jax.tree.map(lambda a: a.astype(jnp.bfloat16) if a.dtype == jnp.float32 else a, shard)


def broadcast(shard, axis, root):
    mine = lax.axis_index(axis) == root
    return lax.psum(jnp.where(mine, shard, jnp.zeros_like(shard)), axis)


def carried_in(shard, axis, join, neutral):
    count = lax.axis_size(axis)
    place = lax.axis_index(axis)
    ahead = count - 1 - place
    gathered = jax.tree.map(
        lambda a, kind: lax.all_gather(a.astype(kind), axis),
        shard,
        jax.tree.map(lambda a: jnp.bfloat16 if a.dtype == jnp.float32 else a.dtype, shard),
    )
    state = jax.tree.map(lambda a, e: jnp.zeros_like(a) + jnp.asarray(e, a.dtype), shard, neutral)

    def one(lap, state):
        source = count - 1 - lap
        return join(
            state,
            jax.tree.map(
                lambda a, own: lax.dynamic_index_in_dim(a, source, 0, False).astype(own.dtype),
                gathered,
                shard,
            ),
        )

    return lax.fori_loop(0, ahead, one, state)


def decay_masks(log_rates):
    cumulative = jnp.cumsum(log_rates, axis=-1)
    width_now = log_rates.shape[-1]
    differ = cumulative[..., :, None] - cumulative[..., None, :]
    lower_part = jnp.arange(width_now)[:, None] >= jnp.arange(width_now)[None, :]
    within = jnp.where(lower_part, jnp.exp(jnp.minimum(differ, 0.0)), 0.0)
    return (cumulative, within)


def group_state(key_rows, value_rows, cumulative):
    weights = jnp.exp(cumulative[..., -1:] - cumulative)[..., None]
    key_gram = jnp.einsum("...sd,...se->...de", key_rows * weights, key_rows, precision=exact_mode)
    value_key = jnp.einsum(
        "...se,...sd->...ed", value_rows * weights, key_rows, precision=exact_mode
    )
    return (cumulative[..., -1], key_gram, value_key)


def group_outputs(
    query_rows, key_rows, value_rows, cumulative, within, key_gram, value_key, ridge_term
):
    entering = jnp.exp(cumulative)[..., None]
    solution = jnp.zeros_like(query_rows)
    residual = query_rows
    direction = query_rows
    norm_now = jnp.sum(residual * residual, axis=-1, keepdims=True)
    for iteration in range(ITERS):
        operator_scores = (
            jnp.einsum("...cd,...sd->...cs", direction, key_rows, precision=exact_mode) * within
        )
        operator_carried = jnp.einsum(
            "...cd,...de->...ce", direction, key_gram, precision=exact_mode
        )
        local_part = jnp.einsum(
            "...cs,...sd->...cd", operator_scores, key_rows, precision=exact_mode
        )
        product = entering * operator_carried + local_part + ridge_term * direction
        step_size = norm_now / (
            jnp.sum(direction * product, axis=-1, keepdims=True) + solve_epsilon
        )
        solution = solution + step_size * direction
        residual = residual - step_size * product
        if iteration + 1 < ITERS:
            norm_next = jnp.sum(residual * residual, axis=-1, keepdims=True)
            direction = residual + norm_next / (norm_now + solve_epsilon) * direction
            norm_now = norm_next
    scores = jnp.einsum("...cd,...sd->...cs", solution, key_rows, precision=exact_mode) * within
    carried = jnp.einsum("...cd,...ed->...ce", solution, value_key, precision=exact_mode)
    return entering * carried + jnp.einsum(
        "...cs,...se->...ce", scores, value_rows, precision=exact_mode
    )


def finish(readout, gain_rows):
    scale_rows = lax.rsqrt(jnp.mean(readout * readout, axis=-1, keepdims=True) + norm_epsilon)
    return (readout * scale_rows * gain_rows).astype(jnp.bfloat16)


def combine(earlier, latter):
    fading = jnp.exp(latter[0])[..., None, None]
    return (
        earlier[0] + latter[0],
        fading * earlier[1] + latter[1],
        fading * earlier[2] + latter[2],
    )


def on_device(queries, key_vectors, value_vectors, log_decay, ridge_shift, norm_gain, out_weight):
    block_len = queries.shape[1]
    local_heads = queries.shape[2] // DK
    group_count = block_len // GROUP

    def split_heads(packed, feature_width):
        return (
            packed.astype(jnp.float32)
            .reshape(2, group_count, GROUP, local_heads, feature_width)
            .transpose(0, 3, 1, 2, 4)
        )

    query_rows = split_heads(queries, DK)
    key_rows = split_heads(key_vectors, DK)
    value_rows = split_heads(value_vectors, DV)
    log_rates = log_decay.reshape(local_heads, 2, group_count, GROUP).transpose(1, 0, 2, 3)
    cumulative, within = decay_masks(log_rates)
    totals, key_grams, value_keys = group_state(key_rows, value_rows, cumulative)
    running = (
        jnp.zeros_like(totals[:, :, 0]),
        jnp.zeros_like(key_grams[:, :, 0]),
        jnp.zeros_like(value_keys[:, :, 0]),
    )
    prefixes = []
    prefixes.append(running)
    running = combine(running, (totals[:, :, 0], key_grams[:, :, 0], value_keys[:, :, 0]))
    first = tuple((member[0] for member in running))
    second = tuple((member[1] for member in running))
    neutral = tuple((jnp.zeros_like(member) for member in first))
    ridge_term = ridge_shift[:, None, None, None]
    gain_rows = norm_gain.reshape(local_heads, 1, 1, DV)

    def solve_row(half_row, entering):
        entering_group = combine(entering, tuple((member[half_row] for member in prefixes[0])))
        gram_list = [entering_group[1]]
        memory_list = [entering_group[2]]
        key_gram = jnp.stack(gram_list, axis=1)
        value_key = jnp.stack(memory_list, axis=1)
        readout = group_outputs(
            query_rows[half_row],
            key_rows[half_row],
            value_rows[half_row],
            cumulative[half_row],
            within[half_row],
            key_gram,
            value_key,
            ridge_term,
        )
        normed = finish(readout, gain_rows)
        return normed.transpose(1, 2, 0, 3).reshape(block_len, local_heads * DV)

    before = entering_2(first, "ctx", combine, neutral)
    front_rows = solve_row(0, before)
    whole_first = jax.tree.map(
        lambda part: broadcast(part, "ctx", lax.axis_size("ctx") - 1),
        for_sending(combine(before, first)),
    )
    from_later = carried_in(second, "ctx", combine, neutral)
    entering_second = combine(whole_first, from_later)
    back_rows = solve_row(1, entering_second)
    flattened = jnp.concatenate([front_rows, back_rows], axis=0)
    columns = out_weight.shape[1]
    mixed_out = jnp.dot(
        lax.all_gather(flattened, "head", axis=1, tiled=True),
        out_weight,
        preferred_element_type=jnp.float32,
    )
    return mixed_out.astype(jnp.bfloat16).reshape(2, block_len, columns)


def solution(mesh):
    return jax.shard_map(
        on_device,
        mesh=mesh,
        in_specs=(
            P(None, "ctx", "head"),
            P(None, "ctx", "head"),
            P(None, "ctx", "head"),
            P("head", None, "ctx"),
            P("head"),
            P("head"),
            P(None, "head"),
        ),
        out_specs=P(None, "ctx", "head"),
        check_vma=False,
    )
```

profile of v0, /device:TPU:0, one launch (start us, length us, event | category | flops | bytes accessed | tf_op | source)
XLA Modules:
  0.0 567.8 jit_solution(12068250197391471740)
XLA Ops:
  13.3 2.7 fusion.67
  17.0 2.7 fusion.64
  27.0 43.1 %all-gather.1 = bf16[16,8,1,1]{1,3,2,0:T(2,128)(2,1)S(1)} all-gather(bf16[1,8,1,1]{1,3,2,0:T(2,128)(2,1)S(1)} %copy.158), channel_id=3, replica_groups=mesh['ctx'=16,'head'=2] {'ctx'}, dimensions={0}, use_global_device_ids=true | all-gather | bytes 272 | tf_op jit(solution)/shard_map/all_gather | solution.py:43
  70.2 36.6 %all-gather = f32[16,8,1,1]{1,3,2,0:T(1,128)S(1)} all-gather(f32[1,8,1,1]{1,3,2,0:T(1,128)S(1)} %copy.137), channel_id=2, replica_groups=mesh['ctx'=16,'head'=2] {'ctx'}, dimensions={0}, use_global_device_ids=true | all-gather | bytes 544 | tf_op jit(solution)/shard_map/all_gather | solution.py:17
  111.0 2.4 exponential_select_fusion
  113.4 18.8 %all-gather.10.cloned.1.call-done = f32[16,8,128,128]{3,2,1,0:T(8,128)} async-done(((f32[1,8,128,128]{3,2,1,0:T(8,128)}), f32[16,8,128,128]{3,2,1,0:T(8,128)}) %all-gather.10.cloned.1.call-update) | async-done | bytes 8388624 | tf_op jit(solution)/shard_map/all_gather | solution.py:17
  132.2 113.3 %all-gather.8.cloned.1.call-done = f32[16,8,128,128]{3,2,1,0:T(8,128)} async-done(((f32[1,8,128,128]{3,2,1,0:T(8,128)}), f32[16,8,128,128]{3,2,1,0:T(8,128)}) %all-gather.8.cloned.1.call-update) | async-done | bytes 8388624 | tf_op jit(solution)/shard_map/all_gather | solution.py:17
  245.6 41.3 %while.33 = (s32[]{:T(128)}, f32[8,128,128]{2,1,0:T(8,128)}, f32[8,128,128]{2,1,0:T(8,128)}, s32[]{:T(128)}, f32[16,8]{1,0:T(8,128)S(1)}, /*index=5*/f32[16,8,12...) while((s32[]{:T(128)}, f32[8,128,128]{2,1,0:T(8,128)}, ...), condition=%wide.region_4.5_spmd.clone, body=%wide.region_3.4_spmd.clone.sunk | while | flops 1048580 | bytes 3145945 | solution.py:26
  245.6 2.4 fusion.128
  248.0 2.8 fusion.128
  250.8 2.8 fusion.128
  253.6 2.8 fusion.128
  256.4 2.8 fusion.128
  259.2 2.8 fusion.128
  262.0 2.8 fusion.128
  264.7 2.8 fusion.128
  267.5 2.8 fusion.128
  270.3 2.8 fusion.128
  273.0 2.8 fusion.128
  275.8 2.8 fusion.128
  278.6 2.8 fusion.128
  281.4 2.8 fusion.128
  284.1 2.8 fusion.128
  286.9 2.6 fusion.106
  289.5 32.6 %all-gather.14.cloned.1.call-done = bf16[16,8,128,128]{3,2,1,0:T(8,128)(2,1)} async-done(((bf16[1,8,128,128]{3,2,1,0:T(8,128)(2,1)}), bf16[16,8,128,128]{3,2,1,0:T(8,128)(2,1)}) %all-gather.14.cloned.1.call-update) | async-done | bytes 4194320 | tf_op jit(solution)/shard_map/all_gather | solution.py:43
  322.1 76.8 %all-gather.12.cloned.1.call-done = bf16[16,8,128,128]{3,2,1,0:T(8,128)(2,1)} async-done(((bf16[1,8,128,128]{3,2,1,0:T(8,128)(2,1)}), bf16[16,8,128,128]{3,2,1,0:T(8,128)(2,1)}) %all-gather.12.cloned.1.call-update) | async-done | bytes 4194320 | tf_op jit(solution)/shard_map/all_gather | solution.py:43
  400.7 38.6 %while.32 = (s32[]{:T(128)}, f32[8]{0:T(128)S(1)}, f32[8,128,128]{2,1,0:T(8,128)}, f32[8,128,128]{2,1,0:T(8,128)}, s32[]{:T(128)}, /*index=5*/bf16[16,8]{1,0:T(8...) while((s32[]{:T(128)}, f32[8]{0:T(128)S(1)}, ...), condition=%wide.region_11.12_spmd, body=%wide.region_10.11_spmd.sunk | while | flops 786454 | bytes 2621755 | solution.py:60
  400.7 2.5 convert_add_fusion.3
  403.3 2.6 convert_add_fusion.3
  405.8 2.6 convert_add_fusion.3
  408.4 2.6 convert_add_fusion.3
  411.0 2.6 convert_add_fusion.3
  413.6 2.6 convert_add_fusion.3
  416.1 2.6 convert_add_fusion.3
  418.7 2.6 convert_add_fusion.3
  421.3 2.6 convert_add_fusion.3
  423.9 2.6 convert_add_fusion.3
  426.5 2.6 convert_add_fusion.3
  429.0 2.6 convert_add_fusion.3
  431.6 2.6 convert_add_fusion.3
  434.2 2.6 convert_add_fusion.3
  436.8 2.6 convert_add_fusion.3
  439.3 2.8 fusion.71
  442.2 69.8 %all-reduce.3.cloned.1.call-done = (bf16[8,128,128]{2,1,0:T(8,128)(2,1)}, bf16[8,128,128]{2,1,0:T(8,128)(2,1)}) async-done(((bf16[8,128,128]{2,1,0:T(8,128)(2,1)}, bf16[8,128,128]{2,1,0:T(8,128)(2,1)}), (bf16[8,128,128]{2,1,0:T(8,128)(2,1)}, bf16[8,128,128]{2,1,0:T(8,128)(2,1)})) %all-reduce.3.cloned.1.call-update) | async-done | bytes 524304 | tf_op jit(solution)/shard_map/psum | solution.py:35
  514.2 2.9 fusion.49
  534.1 2.3 convolution_multiply_fusion
  541.3 9.8 %all-gather.16.cloned.1.call-done = bf16[512,2048]{0,1:T(8,128)(2,1)} async-done(((bf16[512,1024]{0,1:T(8,128)(2,1)}), bf16[512,2048]{0,1:T(8,128)(2,1)}) %all-gather.16.cloned.1.call-update) | async-done | bytes 2097168 | tf_op jit(solution)/shard_map/all_gather | solution.py:193
  551.0 9.9 %convolution_convert_fusion = bf16[512,2048]{1,0:T(8,128)(2,1)} fusion(bf16[512,2048]{0,1:T(8,128)(2,1)} %all-gather.16.cloned.1.call-done, bf16[2048,2048]{1,0:T(8,128)(2,1)} %param.17), kind=kOutput, calls=%fused_computation.15 | convolution fusion | flops 4296015872 | bytes 12582912 | tf_op jit(solution)/shard_map/dot_general | solution.py:192
  (139 shorter events, 45.0 us)
Async XLA Ops:
  6.5 125.7 %all-gather.10.cloned.1.call-start = ((), (), s32[]{:S(2)}) async-start(), calls=%async_computation.1 | async-start | bytes 8912896 | tf_op jit(solution)/shard_map/all_gather | solution.py:17
  13.3 3.6 copy-start.6
  16.0 4.7 copy-start.10
  16.9 228.6 %all-gather.8.cloned.1.call-start = ((), (), s32[]{:S(2)}) async-start(), calls=%async_computation | async-start | bytes 8912896 | tf_op jit(solution)/shard_map/all_gather | solution.py:17
  19.7 4.1 copy-start.11
  20.6 301.5 %all-gather.14.cloned.1.call-start = ((), (), s32[]{:S(2)}) async-start(), calls=%async_computation.3 | async-start | bytes 4456448 | tf_op jit(solution)/shard_map/all_gather | solution.py:43
  21.4 377.6 %all-gather.12.cloned.1.call-start = ((), (), s32[]{:S(2)}) async-start(), calls=%async_computation.2 | async-start | bytes 4456448 | tf_op jit(solution)/shard_map/all_gather | solution.py:43
  22.2 489.7 %all-reduce.3.cloned.1.call-start = ((), (), s32[]{:S(2)}) async-start(), calls=%async_computation.5 | async-start | bytes 1048576 | tf_op jit(solution)/shard_map/psum | solution.py:35
  27.0 80.5 %copy-start.5 = (bf16[2,1,256,8,128]{4,2,3,1,0:T(8,128)(2,1)S(1)}, bf16[2,1,256,8,128]{4,2,3,1,0:T(8,128)(2,1)}, u32[]{:S(2)}) copy-start(bf16[2,1,256,8,128]{4,2,3,1,0:T(8,128)(2,1)} %copy.136) | copy-start | bytes 3145732
  289.5 261.6 %all-gather.16.cloned.1.call-start = ((), (), s32[]{:S(2)}) async-start(), calls=%async_computation.4 | async-start | bytes 3145728 | tf_op jit(solution)/shard_map/all_gather | solution.py:193
  439.3 74.8 %copy-start.15 = (f32[8]{0:T(128)S(1)}, f32[8]{0:T(128)}, u32[]{:S(2)}) copy-start(f32[8]{0:T(128)} %param.15) | copy-start | bytes 100
  512.0 2.1 copy-start.9
  514.1 3.0 copy-start
  514.2 3.5 copy-start.8
  514.2 3.7 copy-start.12
  520.7 1.3 copy-start.1
  520.7 1.3 copy-start.13
  524.1 1.0 copy-start.2
  527.6 1.6 copy-start.4
  532.5 1.6 copy-start.3
  532.5 1.6 copy-start.14
  534.1 2.4 copy-start.7
  537.8 1.3 copy-start.16
Sparse Core Ops, SparseCore 0:
  17.1 115.1 all-gather.9
  135.0 110.5 all-gather.7
  248.3 73.7 all-gather.13
  324.7 74.1 all-gather.11
  404.0 107.9 all-reduce.2
  541.4 9.6 all-gather.15
where the time goes:
time: 569 us; the launch traced here: 568 us
  waiting for transfers between devices  321 us (56%)
  other arithmetic  92.9 us (16%)
  blocking collectives  79.7 us (14%)
  matrix products  44.7 us (8%)
  local copies, waits for them, and re-layouts  14.9 us (3%)
  between operations  14 us (2%)
    all_gather x2, waiting for transfers between devices, entering_2(): pieces = jax.tree.map(lambda part: lax.all_gather(part, axis), value)  132 us
    all_gather x2, waiting for transfers between devices, carried_in(): lax.all_gather(a.astype(kind), axis)  109 us
    psum x1, waiting for transfers between devices, broadcast(): return lax.psum(jnp.where(mine, shard, jnp.zeros_like(shard)), axis)  69.8 us
    all_gather x1, blocking collectives, carried_in(): lax.all_gather(a.astype(kind), axis)  43.1 us
    select_n x15, other arithmetic, lap(): jnp.where(position < mine, new, old)  41.1 us
    add x15, other arithmetic, combine(): fading * earlier[2] + latter[2]  38.4 us
    all_gather x1, blocking collectives, entering_2(): pieces = jax.tree.map(lambda part: lax.all_gather(part, axis), value)  36.6 us
  transfers between devices with their start and end apart: 6, of which 6 were waited for; matrix products, arithmetic and copies ran while one was open for 18% of the time, Pallas kernels for 0%

commit v1 on v0

--- a/solution.py
+++ b/solution.py
@@ -12,6 +12,12 @@
 solve_epsilon = 1e-06
 
 
+def summed_here(x, axis):
+    pieces = lax.all_gather(x, axis, axis=0, tiled=False)
+    result = pieces.sum(axis=0)
+    return result
+
+
 def entering_2(value, axis, join, neutral):
     count, mine = (lax.axis_size(axis), lax.axis_index(axis))
     pieces = jax.tree.map(lambda part: lax.all_gather(part, axis), value)
@@ -32,7 +38,7 @@
 
 def broadcast(shard, axis, root):
     mine = lax.axis_index(axis) == root
-    return lax.psum(jnp.where(mine, shard, jnp.zeros_like(shard)), axis)
+    return summed_here(jnp.where(mine, shard, jnp.zeros_like(shard)), axis)
 
 
 def carried_in(shard, axis, join, neutral):

time: 569 us -> 593 us (1.042)
  waiting for transfers between devices: 321 us -> 351 us
  other arithmetic: 92.9 us -> 79.9 us
    all_gather x0 -> x2, waiting for transfers between devices: none -> 83.3 us  [summed_here(): pieces = lax.all_gather(x, axis, axis=0, tiled=False)]
    psum x1 -> x0, waiting for transfers between devices: 69.8 us -> none  [broadcast(): return lax.psum(jnp.where(mine, shard, jnp.zeros_like(shard)), axis)]
    all_gather x2, waiting for transfers between devices: 132 us -> 180 us  [entering_2(): pieces = jax.tree.map(lambda part: lax.all_gather(part, axis), value)]
    all_gather x2, waiting for transfers between devices: 109 us -> 78.1 us  [carried_in(): lax.all_gather(a.astype(kind), axis)]
    select_n x15, other arithmetic: 41.1 us -> 22.2 us  [lap(): jnp.where(position < mine, new, old)]
    all_gather x1, blocking collectives: 36.6 us -> 43.2 us  [entering_2(): pieces = jax.tree.map(lambda part: lax.all_gather(part, axis), value)]
    reduce_sum x0 -> x2, other arithmetic: none -> 6.04 us  [summed_here(): result = pieces.sum(axis=0)]
  transfers between devices with their start and end apart: 6 -> 7, of which waited for: 6 -> 7; matrix products, arithmetic and copies ran while one was open for 18% -> 19% of each run, Pallas kernels for 0% -> 0%
where the time goes in v1:
time: 593 us; the launch traced here: 592 us
  waiting for transfers between devices  351 us (59%)
  blocking collectives  81.7 us (14%)
  other arithmetic  79.9 us (13%)
  matrix products  49.6 us (8%)
  local copies, waits for them, and re-layouts  15.2 us (3%)
  between operations  14 us (2%)
    all_gather x2, waiting for transfers between devices, entering_2(): pieces = jax.tree.map(lambda part: lax.all_gather(part, axis), value)  180 us
    all_gather x2, waiting for transfers between devices, summed_here(): pieces = lax.all_gather(x, axis, axis=0, tiled=False)  83.3 us
    all_gather x2, waiting for transfers between devices, carried_in(): lax.all_gather(a.astype(kind), axis)  78.1 us
    all_gather x1, blocking collectives, entering_2(): pieces = jax.tree.map(lambda part: lax.all_gather(part, axis), value)  43.2 us
    all_gather x1, blocking collectives, carried_in(): lax.all_gather(a.astype(kind), axis)  38.6 us
    add x15, other arithmetic, combine(): fading * earlier[2] + latter[2]  38.5 us
    select_n x15, other arithmetic, lap(): jnp.where(position < mine, new, old)  22.2 us
  transfers between devices with their start and end apart: 7, of which 7 were waited for; matrix products, arithmetic and copies ran while one was open for 19% of the time, Pallas kernels for 0%

profile of v1, /device:TPU:0, one launch (start us, length us, event | category | flops | bytes accessed | tf_op | source)
XLA Modules:
  0.0 591.8 jit_solution(10801368998767087110)
XLA Ops:
  9.0 1.5 copy.139
  11.1 1.5 copy.142
  13.3 2.7 fusion.67
  16.9 2.7 fusion.64
  22.5 43.2 %all-gather = f32[16,8,1,1]{1,3,2,0:T(1,128)S(1)} all-gather(f32[1,8,1,1]{1,3,2,0:T(1,128)S(1)} %copy.137), channel_id=2, replica_groups=mesh['ctx'=16,'head'=2] {'ctx'}, dimensions={0}, use_global_device_ids=true | all-gather | bytes 544 | tf_op jit(solution)/shard_map/all_gather | solution.py:23
  65.7 66.4 %all-gather.14.cloned.1.call-done = f32[16,8,128,128]{3,2,1,0:T(8,128)} async-done(((f32[1,8,128,128]{3,2,1,0:T(8,128)}), f32[16,8,128,128]{3,2,1,0:T(8,128)}) %all-gather.14.cloned.1.call-update) | async-done | bytes 8388624 | tf_op jit(solution)/shard_map/all_gather | solution.py:23
  132.1 113.3 %all-gather.12.cloned.1.call-done = f32[16,8,128,128]{3,2,1,0:T(8,128)} async-done(((f32[1,8,128,128]{3,2,1,0:T(8,128)}), f32[16,8,128,128]{3,2,1,0:T(8,128)}) %all-gather.12.cloned.1.call-update) | async-done | bytes 8388624 | tf_op jit(solution)/shard_map/all_gather | solution.py:23
  245.3 22.8 %while.33 = (s32[]{:T(128)}, f32[8,128,128]{2,1,0:T(8,128)S(1)}, f32[8,128,128]{2,1,0:T(8,128)S(1)}, s32[]{:T(128)}, f32[16,8]{1,0:T(8,128)S(1)}, /*index=5*/f32...) while((s32[]{:T(128)}, f32[8,128,128]{2,1,0:T(8,128)S(1)}, ...), condition=%wide.region_4.5_spmd.clone, body=%wide.region_3.4_spmd.clone.sunk | while | flops 1048580 | bytes 3145945 | solution.py:32
  253.0 1.5 fusion.128
  254.5 1.5 fusion.128
  263.7 1.5 fusion.128
  268.2 2.4 fusion.106
  270.9 38.6 %all-gather.1 = bf16[16,8,1,1]{1,3,2,0:T(2,128)(2,1)S(1)} all-gather(bf16[1,8,1,1]{1,3,2,0:T(2,128)(2,1)S(1)} %copy.158), channel_id=3, replica_groups=mesh['ctx'=16,'head'=2] {'ctx'}, dimensions={0}, use_global_device_ids=true | all-gather | bytes 272 | tf_op jit(solution)/shard_map/all_gather | solution.py:49
  312.3 1.5 bitcast_convert_fusion
  314.5 1.8 fusion.96
  316.3 1.8 fusion.95
  318.1 2.5 exponential_select_fusion
  321.9 76.9 %all-gather.16.cloned.1.call-done = bf16[16,8,128,128]{3,2,1,0:T(8,128)(2,1)} async-done(((bf16[1,8,128,128]{3,2,1,0:T(8,128)(2,1)}), bf16[16,8,128,128]{3,2,1,0:T(8,128)(2,1)}) %all-gather.16.cloned.1.call-update) | async-done | bytes 4194320 | tf_op jit(solution)/shard_map/all_gather | solution.py:49
  400.5 38.7 %while.32 = (s32[]{:T(128)}, f32[8]{0:T(128)S(1)}, f32[8,128,128]{2,1,0:T(8,128)}, f32[8,128,128]{2,1,0:T(8,128)}, s32[]{:T(128)}, /*index=5*/bf16[16,8]{1,0:T(8...) while((s32[]{:T(128)}, f32[8]{0:T(128)S(1)}, ...), condition=%wide.region_11.12_spmd, body=%wide.region_10.11_spmd.sunk | while | flops 786454 | bytes 2621755 | solution.py:66
  400.5 2.6 convert_add_fusion.3
  403.1 2.6 convert_add_fusion.3
  405.7 2.6 convert_add_fusion.3
  408.3 2.6 convert_add_fusion.3
  410.9 2.6 convert_add_fusion.3
  413.4 2.6 convert_add_fusion.3
  416.0 2.6 convert_add_fusion.3
  418.6 2.6 convert_add_fusion.3
  421.2 2.6 convert_add_fusion.3
  423.7 2.6 convert_add_fusion.3
  426.3 2.6 convert_add_fusion.3
  428.9 2.6 convert_add_fusion.3
  431.5 2.6 convert_add_fusion.3
  434.1 2.6 convert_add_fusion.3
  436.6 2.6 convert_add_fusion.3
  439.2 2.8 fusion.71
  442.0 33.6 %all-gather.22.cloned.1.call-done = bf16[128,128,128]{2,1,0:T(8,128)(2,1)} async-done(((bf16[8,128,128]{2,1,0:T(8,128)(2,1)}), bf16[128,128,128]{2,1,0:T(8,128)(2,1)}) %all-gather.22.cloned.1.call-update) | async-done | bytes 4194320 | tf_op jit(solution)/shard_map/all_gather | solution.py:16
  475.6 3.0 reduce_sum.120
  478.7 2.0 fusion.70
  480.8 2.9 fusion.49
  495.3 2.5 convolution_multiply_fusion.3
  497.8 2.5 fusion.97
  500.3 2.5 fusion.100
  502.8 49.7 %all-gather.24.cloned.1.call-done = bf16[128,128,128]{2,1,0:T(8,128)(2,1)} async-done(((bf16[8,128,128]{2,1,0:T(8,128)(2,1)}), bf16[128,128,128]{2,1,0:T(8,128)(2,1)}) %all-gather.24.cloned.1.call-update) | async-done | bytes 4194320 | tf_op jit(solution)/shard_map/all_gather | solution.py:16
  552.5 3.1 reduce_sum.124
  555.6 3.0 convolution_multiply_fusion
  558.7 3.1 multiply_reduce_fusion
  565.7 9.3 %all-gather.20.cloned.1.call-done = bf16[512,2048]{0,1:T(8,128)(2,1)} async-done(((bf16[512,1024]{0,1:T(8,128)(2,1)}), bf16[512,2048]{0,1:T(8,128)(2,1)}) %all-gather.20.cloned.1.call-update) | async-done | bytes 2097168 | tf_op jit(solution)/shard_map/all_gather | solution.py:199
  575.1 9.9 %convolution_convert_fusion = bf16[512,2048]{1,0:T(8,128)(2,1)} fusion(bf16[512,2048]{0,1:T(8,128)(2,1)} %all-gather.20.cloned.1.call-done, bf16[2048,2048]{1,0:T(8,128)(2,1)} %param.17), kind=kOutput, calls=%fused_computation.15 | convolution fusion | flops 4296015872 | bytes 12582912 | tf_op jit(solution)/shard_map/dot_general | solution.py:198
  (152 shorter events, 47.8 us)
Async XLA Ops:
  6.5 125.5 %all-gather.14.cloned.1.call-start = ((), (), s32[]{:S(2)}) async-start(), calls=%async_computation.1 | async-start | bytes 8912896 | tf_op jit(solution)/shard_map/all_gather | solution.py:23
  13.3 3.5 copy-start.10
  16.9 228.5 %all-gather.12.cloned.1.call-start = ((), (), s32[]{:S(2)}) async-start(), calls=%async_computation | async-start | bytes 8912896 | tf_op jit(solution)/shard_map/all_gather | solution.py:23
  19.6 2.6 copy-start.16
  20.5 301.4 %all-gather.18.cloned.1.call-start = ((), (), s32[]{:S(2)}) async-start(), calls=%async_computation.3 | async-start | bytes 4456448 | tf_op jit(solution)/shard_map/all_gather | solution.py:49
  21.3 377.5 %all-gather.16.cloned.1.call-start = ((), (), s32[]{:S(2)}) async-start(), calls=%async_computation.2 | async-start | bytes 4456448 | tf_op jit(solution)/shard_map/all_gather | solution.py:49
  22.2 453.5 %all-gather.22.cloned.1.call-start = ((), (), s32[]{:S(2)}) async-start(), calls=%async_computation.5 | async-start | bytes 4456448 | tf_op jit(solution)/shard_map/all_gather | solution.py:16
  268.2 42.7 %copy-start.5 = (f32[8,128,128]{2,1,0:T(8,128)}, f32[8,128,128]{2,1,0:T(8,128)S(1)}, u32[]{:S(2)}) copy-start(f32[8,128,128]{2,1,0:T(8,128)S(1)} %get-tuple-element.236) | copy-start | bytes 1572868
  268.2 42.7 %copy-start.7 = (f32[8,128,128]{2,1,0:T(8,128)}, f32[8,128,128]{2,1,0:T(8,128)S(1)}, u32[]{:S(2)}) copy-start(f32[8,128,128]{2,1,0:T(8,128)S(1)} %get-tuple-element.237) | copy-start | bytes 1572868
  270.7 281.8 %all-gather.24.cloned.1.call-start = ((), (), s32[]{:S(2)}) async-start(), calls=%async_computation.6 | async-start | bytes 4456448 | tf_op jit(solution)/shard_map/all_gather | solution.py:16
  312.3 2.2 copy-start.9
  320.6 254.4 %all-gather.20.cloned.1.call-start = ((), (), s32[]{:S(2)}) async-start(), calls=%async_computation.4 | async-start | bytes 3145728 | tf_op jit(solution)/shard_map/all_gather | solution.py:199
  478.6 2.1 copy-start.13
  478.6 2.1 copy-start.19
  480.7 3.0 copy-start
  480.7 3.5 copy-start.12
  480.8 3.7 copy-start.17
  487.1 1.3 copy-start.4
  488.4 11.9 %copy-start.2 = (f32[8,256,128]{2,1,0:T(8,128)}, f32[8,256,128]{2,1,0:T(8,128)S(1)}, u32[]{:S(2)}) copy-start(f32[8,256,128]{2,1,0:T(8,128)S(1)} %get-tuple-element.387) | copy-start | bytes 3145732
  490.5 1.3 copy-start.6
  494.0 1.3 copy-start.8
  552.5 3.1 copy-start.3
  555.6 3.1 copy-start.11
  555.6 3.1 copy-start.15
  555.6 6.2 %copy-start.18 = (f32[8,256,128]{2,1,0:T(8,128)S(1)}, f32[8,256,128]{2,1,0:T(8,128)}, u32[]{:S(2)}) copy-start(f32[8,256,128]{2,1,0:T(8,128)} %convolution_multiply_fusion.3) | copy-start | bytes 3145732
  558.7 3.1 copy-start.1
  558.7 3.5 copy-start.14
  562.2 1.3 copy-start.20
Sparse Core Ops, SparseCore 0:
  17.0 115.0 all-gather.13
  134.8 110.4 all-gather.11
  248.1 73.7 all-gather.17
  324.6 74.1 all-gather.15
  401.4 74.1 all-gather.21
  478.3 74.1 all-gather.23
  565.9 9.1 all-gather.19
